TPU v7x, 32 devices: a whole 2x2x4 slice. The times are simulated.
32 devices in a mesh: groups: 2 (over y), row: 8 (over z, x), col: 2 (over core).
Axes of the slice: x: 2, y: 2, z: 4, core: 2. Of those that a mesh axis runs over, the one named last changes fastest.
Arguments:
- sigma_anc: bfloat16 [16384, 8192], P(('groups', 'row'), 'col'), parts along dimension 0, as said below
- panel: bfloat16 [16384, 3072], P(('groups', 'row'), 'col'), parts along dimension 0
- holder: int32 [128], P('groups'), parts along dimension 0, may hold values from 0 to 63, each once
- dinv_diag: float32 [6144], P(('groups', 'col')), parts along dimension 0, may hold values from 0.5 to 2
Outputs:
- sigma_aj: bfloat16 [16384, 3072], P(('groups', 'row'), 'col'), parts along dimension 0
- variances: float32 [6144], P(('groups', 'col')), parts along dimension 0
There are 2 independent parts, one for each index of `groups`. A program takes and returns all parts, laid end to end along the dimension named above; each array names one. Nothing has to cross between parts.
Inputs may be any that keep to these rules, and one draw needn't show every extreme that they name: holder is a permutation of the 64 tiles. sigma_anc is symmetric and positive definite.
All inputs are finite; a program needn't handle non-finite values.
Results may differ from a plain program's by a relative error of at most 0.001.
Values may be sent and summed in bfloat16 or wider, within the bound.
A program may use at most 128 MiB of HBM per device.

v0:
```python
import functools

import jax
import jax.numpy as jnp
from jax import lax
from jax.experimental import pallas as pl
from jax.experimental.pallas import tpu as pltpu
from jax.sharding import PartitionSpec as P

MESH = pl.DeviceIdType.MESH


def block_of(size, most):
    block = min(size, most)
    while size % block:
        block -= 128
    return block


def kernel(n, nc, holder, logical, sigma, panel, out, sums, s, p, acc, staged, parts,
           own_sem, far_sem, near_sem, f_send, f_recv, b_send, b_recv, o_sem, v_send, v_recv):
    g = lax.axis_index("groups")
    r = lax.axis_index("row")
    c = lax.axis_index("col")
    per, tile, cols = panel.shape
    rows, width = sigma.shape
    tiles = p.shape[0]
    half = n // 2
    fwd = (per + 1) // 2
    bwd = per - fwd

    def row_of(at):
        at = lax.rem(at + 2 * n, n)
        odd = at // half
        return 2 * (at + odd * (2 * half - 1 - 2 * at)) + odd

    odd = lax.rem(r, 2)
    up = r // 2
    at = up + odd * (2 * half - 1 - 2 * up)
    after = (g, row_of(at + 1), c)
    before = (g, row_of(at - 1), c)

    barrier = pltpu.get_barrier_semaphore()

    def greet(k, carry):
        pl.semaphore_signal(barrier, 1, device_id=(g, lax.rem(r + k, n), c), device_id_type=MESH)
        return carry

    lax.fori_loop(1, n, greet, 0)
    for k in range(1, nc):
        pl.semaphore_signal(barrier, 1, device_id=(g, r, lax.rem(c + k, nc)), device_id_type=MESH)
    pl.semaphore_wait(barrier, n - 1 + nc - 1)

    def f_tile(k, i):
        return row_of(at - k) * per + i

    def b_tile(k, i):
        return row_of(at + k) * per + fwd + i

    def f_copy(k, i, src=None):
        t = f_tile(k, i)
        return pltpu.make_async_remote_copy(
            src_ref=p.at[t] if src is None else src, dst_ref=p.at[t],
            send_sem=f_send.at[k * fwd + i], recv_sem=f_recv.at[k * fwd + i],
            device_id=after, device_id_type=MESH)

    def b_copy(k, i, src=None):
        t = b_tile(k, i)
        return pltpu.make_async_remote_copy(
            src_ref=p.at[t] if src is None else src, dst_ref=p.at[t],
            send_sem=b_send.at[k * bwd + i], recv_sem=b_recv.at[k * bwd + i],
            device_id=before, device_id_type=MESH)

    def f_landed(k, i):
        t = f_tile(k, i)
        return pltpu.make_async_remote_copy(
            src_ref=p.at[t], dst_ref=p.at[t],
            send_sem=f_send.at[(k - 1) * fwd + i], recv_sem=f_recv.at[(k - 1) * fwd + i],
            device_id=after, device_id_type=MESH)

    def b_landed(k, i):
        t = b_tile(k, i)
        return pltpu.make_async_remote_copy(
            src_ref=p.at[t], dst_ref=p.at[t],
            send_sem=b_send.at[(k - 1) * bwd + i], recv_sem=b_recv.at[(k - 1) * bwd + i],
            device_id=before, device_id_type=MESH)

    for i in range(fwd):
        f_copy(0, i, panel.at[i]).start()
        if i < bwd:
            b_copy(0, i, panel.at[fwd + i]).start()

    held = width // tile

    def near(j):
        return pltpu.make_async_copy(
            sigma.at[:, pl.ds(pl.multiple_of(j * tile, tile), tile)], s.at[c * held + j], near_sem.at[j])

    def far(k, j):
        return pltpu.make_async_remote_copy(
            src_ref=sigma.at[:, pl.ds(pl.multiple_of(j * tile, tile), tile)], dst_ref=s.at[c * held + j],
            send_sem=far_sem.at[2 * k - 2, j], recv_sem=far_sem.at[2 * k - 1, j],
            device_id=(g, r, lax.rem(c + k, nc)), device_id_type=MESH)

    def far_landed(k, j):
        t = lax.rem(c + nc - k, nc) * held + j
        return pltpu.make_async_remote_copy(
            src_ref=s.at[t], dst_ref=s.at[t],
            send_sem=far_sem.at[2 * k - 2, j], recv_sem=far_sem.at[2 * k - 1, j],
            device_id=(g, r, lax.rem(c + k, nc)), device_id_type=MESH)

    def each(low, high, act):
        def step(k, carry):
            act(k)
            return carry
        lax.fori_loop(low, high, step, 0)

    for k in range(1, nc):
        each(0, held, lambda j: far(k, j).start())
    each(0, held, lambda j: near(j).start())
    own = pltpu.make_async_copy(panel, p.at[pl.ds(r * per, per)], own_sem)
    own.start()
    acc[...] = jnp.zeros_like(acc)
    own.wait()
    each(0, held, lambda j: near(j).wait())
    for k in range(1, nc):
        each(0, held, lambda j: far_landed(k, j).wait_recv())

    rb = block_of(rows, 512)
    cb = block_of(cols, 512)
    across = cols // cb

    def multiply(slots):
        columns = [logical[t] for t in slots]

        def block(q, carry):
            rs = pl.ds(pl.multiple_of((q // across) * rb, rb), rb)
            cs = pl.ds(pl.multiple_of(lax.rem(q, across) * cb, cb), cb)
            lhs = jnp.concatenate([s[w, rs, :] for w in columns], axis=1)
            rhs = jnp.concatenate([p[t, :, cs] for t in slots], axis=0)
            acc[rs, cs] += jnp.dot(lhs, rhs, preferred_element_type=jnp.float32)
            return carry

        lax.fori_loop(0, (rows // rb) * across, block, 0)

    def unit(u, carry):
        k = u // fwd
        i = lax.rem(u, fwd)

        @pl.when(k > 0)
        def _():
            f_landed(k, i).wait_recv()

            @pl.when(k < n - 1)
            def _():
                f_copy(k, i).start()

        if bwd == fwd:
            @pl.when(k > 0)
            def _():
                b_landed(k, i).wait_recv()

                @pl.when(k < n - 1)
                def _():
                    b_copy(k, i).start()

            multiply([f_tile(k, i), b_tile(k, i)])
        else:
            multiply([f_tile(k, i)])
            if bwd:
                @pl.when(i < bwd)
                def _():
                    @pl.when(k > 0)
                    def _():
                        b_landed(k, i).wait_recv()

                        @pl.when(k < n - 1)
                        def _():
                            b_copy(k, i).start()

                    multiply([b_tile(k, i)])
        return carry

    lax.fori_loop(0, n * fwd, unit, 0)

    parts[r] = jnp.zeros((1, cols), jnp.float32)

    def weigh(j, carry):
        where = pl.ds(pl.multiple_of(j * tile, tile), tile)
        mine = p[holder[r * per + j]]
        for b in range(across):
            cs = pl.ds(b * cb, cb)
            term = mine[:, b * cb:(b + 1) * cb].astype(jnp.float32) * acc[where, cs]
            parts[r, :, cs] += jnp.sum(term, axis=0, keepdims=True)
        return carry

    lax.fori_loop(0, per, weigh, 0)

    def share(k):
        to = lax.rem(r + k, n)
        return pltpu.make_async_remote_copy(
            src_ref=parts.at[r], dst_ref=parts.at[r],
            send_sem=v_send.at[k - 1], recv_sem=v_recv.at[k - 1],
            device_id=(g, to, c), device_id_type=MESH)

    def gone(k):
        frm = lax.rem(r + n - k, n)
        return pltpu.make_async_remote_copy(
            src_ref=parts.at[frm], dst_ref=parts.at[frm],
            send_sem=v_send.at[k - 1], recv_sem=v_recv.at[k - 1],
            device_id=(g, lax.rem(r + k, n), c), device_id_type=MESH)

    each(1, n, lambda k: share(k).start())

    def put(j):
        where = pl.ds(pl.multiple_of(j * tile, tile), tile)
        return pltpu.make_async_copy(staged.at[where], out.at[where], o_sem.at[j])

    def finish(j, carry):
        where = pl.ds(pl.multiple_of(j * tile, tile), tile)
        staged[where, :] = (-acc[where, :]).astype(staged.dtype)
        put(j).start()
        return carry

    lax.fori_loop(0, per, finish, 0)

    for k in range(1, nc):
        each(0, held, lambda j: far(k, j).wait_send())
    each(0, (n - 1) * fwd, lambda u: f_copy(u // fwd, lax.rem(u, fwd)).wait_send())
    if bwd:
        each(0, (n - 1) * bwd, lambda u: b_copy(u // bwd, lax.rem(u, bwd)).wait_send())
    each(0, per, lambda j: put(j).wait())
    each(1, n, lambda k: gone(k).wait_recv())
    each(1, n, lambda k: share(k).wait_send())
    total = parts[0]
    for k in range(1, n):
        total += parts[k]
    sums[...] = total


def body(n, nc, sigma_anc, panel, holder, dinv_diag):
    tiles = holder.shape[0]
    rows, width = sigma_anc.shape
    cols = panel.shape[1]
    per = tiles // n
    tile = panel.shape[0] // per
    fwd = (per + 1) // 2
    bwd = max(per - fwd, 1)
    ids = jnp.arange(tiles, dtype=jnp.int32)
    logical = jnp.sum(jnp.where(holder[:, None] == ids[None, :], ids[:, None], 0), axis=0, dtype=jnp.int32)
    dma = pltpu.SemaphoreType.DMA
    out, sums = pl.pallas_call(
        functools.partial(kernel, n, nc),
        out_shape=(
            jax.ShapeDtypeStruct((rows, cols), jnp.bfloat16),
            jax.ShapeDtypeStruct((1, cols), jnp.float32),
        ),
        in_specs=[
            pl.BlockSpec(memory_space=pltpu.SMEM),
            pl.BlockSpec(memory_space=pltpu.SMEM),
            pl.BlockSpec(memory_space=pl.ANY),
            pl.BlockSpec(memory_space=pl.ANY),
        ],
        out_specs=(
            pl.BlockSpec(memory_space=pl.ANY),
            pl.BlockSpec(memory_space=pltpu.VMEM),
        ),
        scratch_shapes=[
            pltpu.VMEM((width * nc // tile, rows, tile), sigma_anc.dtype),
            pltpu.VMEM((tiles, tile, cols), panel.dtype),
            pltpu.VMEM((rows, cols), jnp.float32),
            pltpu.VMEM((rows, cols), jnp.bfloat16),
            pltpu.VMEM((n, 1, cols), jnp.float32),
            dma,
            dma((2 * nc, width // tile)),
            dma((width // tile,)),
            dma((n * fwd,)),
            dma((n * fwd,)),
            dma((n * bwd,)),
            dma((n * bwd,)),
            dma((per,)),
            dma((n,)),
            dma((n,)),
        ],
        compiler_params=pltpu.CompilerParams(
            collective_id=0, has_side_effects=True, vmem_limit_bytes=60 << 20
        ),
    )(holder, logical, sigma_anc, panel.reshape(per, tile, cols))
    return out, dinv_diag + sums.reshape(cols)


def solution(mesh):
    placed = (
        P(("groups", "row"), "col"),
        P(("groups", "row"), "col"),
        P("groups"),
        P(("groups", "col")),
    )
    return jax.shard_map(
        functools.partial(body, mesh.shape["row"], mesh.shape["col"]),
        mesh=mesh,
        in_specs=placed,
        out_specs=(P(("groups", "row"), "col"), P(("groups", "col"))),
        check_vma=False,
    )
```

profile of v0, /device:TPU:0, one launch (start us, length us, event | category | flops | bytes accessed | tf_op | source)
XLA Modules:
  0.0 260.5 jit_solution(843686129106529932)
XLA Ops:
  0.6 1.3 select_reduce_fusion.logical
  1.9 0.0 copy-start
  1.9 253.5 %shard_map.59 = (bf16[1024,1536]{1,0:T(8,128)(2,1)}, f32[1,1536]{1,0:T(1,128)}) custom-call(s32[64]{0:T(128)} %holder.1, s32[64]{0:T(128)} %select_reduce_fusion.logical, bf16[1024,4096]{1,0:T(8,128)(2,1)} %sigma.1, bf16[8,128,1536]{2,1,0:T(8,128)(2,1)} %bitcast.1), custom_call_target="tpu_custom_call" | custom-call | tf_op jit(solution)/shard_map/pallas_call | solution.py:252
  255.4 0.7 reduce
  256.1 0.0 copy-done
  256.1 0.6 add.3
  256.7 3.8 %copy.7 = bf16[1024,1536]{1,0:T(8,128)(2,1)} copy(bf16[1024,1536]{1,0:T(8,128)(2,1)} %get-tuple-element.8) | data formatting | bytes 6291456
Async XLA Ops:
  1.9 254.2 %copy-start = (f32[1536]{0:T(1024)S(1)}, f32[1536]{0:T(1024)}, u32[]{:S(2)}) copy-start(f32[1536]{0:T(1024)} %param.7) | copy-start | bytes 18436
where the time goes:
time: 261 us; the launch traced here: 260 us
  Pallas kernels  253 us (97%)
  local copies, waits for them, and re-layouts  3.76 us (1%)
    pallas_call x1, Pallas kernels, body(): pl.pallas_call(functools.partial(kernel, n, nc), out_shape=(jax.ShapeDtyp...  253 us

commit v1 on v0

--- a/solution.py
+++ b/solution.py
@@ -238,6 +238,418 @@
     sums[...] = total
 
 
+def ladder(n, nc, wide, split, spare, kept, holder, logical, sigma, panel, out, sums,
+           s, acc, staged, ef, accf, across, along, parts,
+           far_sem, near_sem, own_sem, p_send, p_recv, u_send, u_recv, w_send, w_recv,
+           t_send, t_recv, y_send, y_recv, e_send, e_recv, o_sem, v_send, v_recv, *bufs):
+    g = lax.axis_index("groups")
+    r = lax.axis_index("row")
+    c = lax.axis_index("col")
+    per, tile, cols = panel.shape
+    rows, width = sigma.shape
+    chunks = cols // wide
+    ps, ses = bufs[:chunks], bufs[chunks:]
+    held = width // tile
+    grp = per // split
+    steps = chunks * split
+    late = spare * split
+    z = r // 2
+    x = lax.rem(r, 2)
+    xb = 1 - x
+    side = z // 2
+    ze, zm, zo, zf = 3 * side, 1 + side, 2 - side, 3 - 3 * side
+    edge = 2 * ze + x
+
+    def at(zz, xx):
+        return 2 * zz + xx
+
+    def dev(zz, xx):
+        return (g, 2 * zz + xx, c)
+
+    twin = (g, r, 1 - c)
+
+    barrier = pltpu.get_barrier_semaphore()
+
+    def greet(k, carry):
+        pl.semaphore_signal(barrier, 1, device_id=(g, lax.rem(r + k, n), c), device_id_type=MESH)
+        return carry
+
+    lax.fori_loop(1, n, greet, 0)
+    pl.semaphore_signal(barrier, 1, device_id=twin, device_id_type=MESH)
+    pl.semaphore_wait(barrier, n)
+
+    def each(low, high, act):
+        def step(k, carry):
+            act(k)
+            return carry
+        lax.fori_loop(low, high, step, 0)
+
+    def piece(block, i):
+        return ps[i // split].at[pl.ds(block * per + (i % split) * grp, grp)]
+
+    def first(i):
+        return panel.at[pl.ds((i % split) * grp, grp), :, pl.ds((i // split) * wide, wide)]
+
+    def move(block, i, to, way, src=None):
+        return pltpu.make_async_remote_copy(
+            src_ref=piece(block, i) if src is None else src, dst_ref=piece(block, i),
+            send_sem=p_send.at[block, way, i], recv_sem=p_recv.at[block, i],
+            device_id=to, device_id_type=MESH)
+
+    def near(j):
+        return pltpu.make_async_copy(
+            sigma.at[:, pl.ds(pl.multiple_of(j * tile, tile), tile)], s.at[c * held + j], near_sem.at[j])
+
+    def far(j):
+        return pltpu.make_async_remote_copy(
+            src_ref=sigma.at[:, pl.ds(pl.multiple_of(j * tile, tile), tile)], dst_ref=s.at[c * held + j],
+            send_sem=far_sem.at[0, j], recv_sem=far_sem.at[1, j], device_id=twin, device_id_type=MESH)
+
+    def far_landed(j):
+        t = (1 - c) * held + j
+        return pltpu.make_async_remote_copy(
+            src_ref=s.at[t], dst_ref=s.at[t],
+            send_sem=far_sem.at[0, j], recv_sem=far_sem.at[1, j], device_id=twin, device_id_type=MESH)
+
+    def own(q):
+        return pltpu.make_async_copy(
+            panel.at[:, :, pl.ds(q * wide, wide)], ps[q].at[pl.ds(r * per, per)], own_sem.at[q])
+
+    def load_sigma():
+        each(0, held, lambda j: far(j).start())
+        each(0, held, lambda j: near(j).start())
+        for q in range(chunks):
+            own(q).start()
+
+    def have_sigma():
+        each(0, held, lambda j: near(j).wait())
+        each(0, held, lambda j: far_landed(j).wait_recv())
+        for q in range(chunks):
+            own(q).wait()
+        parts[r] = jnp.zeros((1, cols), jnp.float32)
+
+    rb = block_of(rows, 512)
+
+    def multiply(i):
+        q, h = i // split, i % split
+        if h == 0:
+            acc[...] = jnp.zeros_like(acc)
+        downs = rows // rb
+
+        def block(u, carry):
+            pair = u // downs
+            rs = pl.ds(pl.multiple_of(lax.rem(u, downs) * rb, rb), rb)
+            slots = [(2 * pair + m) * per + h * grp + j for m in range(2) for j in range(grp)]
+            lhs = jnp.concatenate([s[logical[t], rs, :] for t in slots], axis=1)
+            rhs = jnp.concatenate([ps[q][t] for t in slots], axis=0)
+            acc[rs, :] += jnp.dot(lhs, rhs, preferred_element_type=jnp.float32)
+            return carry
+
+        lax.fori_loop(0, (n // 2) * downs, block, 0)
+
+    def put(q):
+        return pltpu.make_async_copy(
+            staged.at[q % 2], out.at[:, pl.ds(q * wide, wide)], o_sem.at[q])
+
+    def finish(q, waited):
+        cs = pl.ds(q * wide, wide)
+
+        if waited is not None:
+            put(waited).wait()
+
+        def weigh(j, carry):
+            where = pl.ds(pl.multiple_of(j * tile, tile), tile)
+            prod = acc[where, :]
+            staged[q % 2, where, :] = (-prod).astype(staged.dtype)
+            term = ps[q][holder[r * per + j]].astype(jnp.float32) * prod
+            parts[r, :, cs] += jnp.sum(term, axis=0, keepdims=True)
+            return carry
+
+        lax.fori_loop(0, per, weigh, 0)
+        put(q).start()
+
+    def rel(idx):
+        zz = idx // 2
+        base = jnp.where(zz == 0, 1, jnp.where(zz == 1, 2, jnp.where(zz == 2, 0, 3)))
+        return 2 * (base + side * (3 - 2 * base)) + lax.rem(x + idx, 2)
+
+    same = [(k, d) for k in range(per) for d in (([1] if k >= kept else []) + [4, 5])]
+    other = [(k, d) for k in range(per) for d in (([2] if k >= kept else []) + [3, 6, 7])]
+    quota = -(-max(len(same), len(other)) // (steps + 1))
+
+    def turn(u):
+        return min(u // quota, steps)
+
+    def unit(k, d, to):
+        b = rel(d)
+        return pltpu.make_async_remote_copy(
+            src_ref=sigma.at[pl.ds(k * tile, tile), pl.ds(pl.multiple_of((b - c * (n // nc)) * rows, rows), rows)],
+            dst_ref=ses[k].at[:, pl.ds(pl.multiple_of(b * rows, rows), rows)],
+            send_sem=u_send.at[k, d], recv_sem=u_recv.at[k, d], device_id=to, device_id_type=MESH)
+
+    def pass_on(k, d):
+        b = rel(d)
+        ref = ses[k].at[:, pl.ds(pl.multiple_of(b * rows, rows), rows)]
+        return pltpu.make_async_remote_copy(
+            src_ref=ref, dst_ref=ref, send_sem=w_send.at[k, d], recv_sem=w_recv.at[k, d],
+            device_id=twin, device_id_type=MESH)
+
+    def by_core(act):
+        @pl.when(c == side)
+        def _():
+            act(same, other)
+
+        @pl.when(c != side)
+        def _():
+            act(other, same)
+
+    half = rows // nc
+
+    def lend(k, way):
+        dst = (across, along)[way].at[k, pl.ds(pl.multiple_of(c * half, half), half)]
+        who = (at(ze, xb), at(zf, x))[way]
+        return pltpu.make_async_remote_copy(
+            src_ref=s.at[who * per + k, pl.ds(pl.multiple_of(c * half, half), half)], dst_ref=dst,
+            send_sem=t_send.at[way, k], recv_sem=t_recv.at[way, k],
+            device_id=(dev(zm, xb), dev(zo, x))[way], device_id_type=MESH)
+
+    def lend_on(k, way, core):
+        ref = (across, along)[way].at[k, pl.ds(pl.multiple_of(core * half, half), half)]
+        return pltpu.make_async_remote_copy(
+            src_ref=ref, dst_ref=ref, send_sem=y_send.at[way, k], recv_sem=y_recv.at[way, k],
+            device_id=twin, device_id_type=MESH)
+
+    def back(k):
+        ref = ef.at[pl.ds(k * tile, tile)]
+        return pltpu.make_async_remote_copy(
+            src_ref=ref, dst_ref=ref, send_sem=e_send.at[k], recv_sem=e_recv.at[k],
+            device_id=dev(ze, x), device_id_type=MESH)
+
+    def for_edge(k):
+        def landed(mine, theirs):
+            for kk, d in theirs:
+                if kk == k:
+                    pass_on(k, d).wait_recv()
+
+        by_core(landed)
+        if k < kept:
+            for way in range(2):
+                lend_on(k, way, 1 - c).wait_recv()
+        turned = [(s.at[edge * per + k], r)]
+        if k < kept:
+            turned += [(across.at[k], at(zm, xb)), (along.at[k], at(zo, x))]
+        accf[...] = jnp.zeros_like(accf)
+
+        def rhs(q, b):
+            return jnp.concatenate([ps[q][holder[b * per + j]] for j in range(per)], axis=0)
+
+        for ref, b in turned:
+            for q in range(spare):
+                cs = pl.ds(q * wide, wide)
+                accf[:, cs] += lax.dot_general(
+                    ref[...], rhs(q, b), (((0,), (0,)), ((), ())), preferred_element_type=jnp.float32)
+
+        def straight(d, carry):
+            b = rel(d)
+            lhs = ses[k][:, pl.ds(pl.multiple_of(b * rows, rows), rows)]
+            for q in range(spare):
+                cs = pl.ds(q * wide, wide)
+                accf[:, cs] += jnp.dot(lhs, rhs(q, b), preferred_element_type=jnp.float32)
+            return carry
+
+        lax.fori_loop(3 if k < kept else 1, n, straight, 0)
+        ef[pl.ds(k * tile, tile), :] = (-accf[...]).astype(ef.dtype)
+        for q in range(spare):
+            cs = pl.ds(q * wide, wide)
+            term = ps[q][holder[edge * per + k]].astype(jnp.float32) * accf[:, cs]
+            parts[r, :, cs] += jnp.sum(term, axis=0, keepdims=True)
+        back(k).start()
+
+    def middle():
+        sent = []
+
+        def go(copy):
+            copy.start()
+            sent.append(copy)
+
+        ready = {}
+        for k in range(per):
+            last = max(turn(max(u for u, (kk, _) in enumerate(lst) if kk == k)) for lst in (same, other))
+            ready.setdefault(max(last + 2, late + 3 + k, 4 + k), []).append(k)
+        total = max(steps + 3, max(ready) + 1)
+        waited = None
+        for i in range(total):
+            if i < steps:
+                go(move(r, i, dev(zm, xb), 0, first(i)))
+                go(move(r, i, dev(zo, x), 1, first(i)))
+                if i >= late:
+                    go(move(r, i, dev(ze, x), 2, first(i)))
+            if i == 0:
+                load_sigma()
+            if i == 2:
+                have_sigma()
+            j = i - 1
+            if 0 <= j < steps:
+                b = at(ze, x)
+                move(b, j, twin, 0).wait_recv()
+                go(move(b, j, dev(zm, xb), 0))
+                go(move(b, j, dev(zo, x), 1))
+                b = at(zm, xb)
+                move(b, j, twin, 0).wait_recv()
+                go(move(b, j, dev(zo, x), 1))
+                b = at(zo, x)
+                move(b, j, twin, 0).wait_recv()
+                if j >= late:
+                    go(move(b, j, dev(ze, x), 2))
+            j = i - 2
+            if 0 <= j < steps:
+                b = at(zf, x)
+                move(b, j, twin, 0).wait_recv()
+                go(move(b, j, dev(zm, xb), 0))
+                if j >= late:
+                    go(move(b, j, dev(ze, x), 2))
+                move(at(ze, xb), j, twin, 0).wait_recv()
+                move(at(zo, xb), j, twin, 0).wait_recv()
+            k = i - 2
+            if 0 <= k < kept:
+                for way in range(2):
+                    go(lend(k, way))
+            k = i - 3
+            if 0 <= k < kept:
+                for way in range(2):
+                    lend(k, way).wait_recv()
+                    go(lend_on(k, way, c))
+            j = i - 2
+
+            def relay(mine, theirs):
+                for u, (k, d) in enumerate(mine):
+                    if turn(u) == j:
+                        unit(k, d, twin).wait_recv()
+                        pass_on(k, d).start()
+
+            by_core(relay)
+            j = i - 3
+            if 0 <= j < steps:
+                move(at(zf, xb), j, twin, 0).wait_recv()
+                multiply(j)
+                if j % split == split - 1:
+                    q = j // split
+                    finish(q, q - 2 if q >= 2 else None)
+            for k in ready.get(i, ()):
+                for_edge(k)
+
+        for k in range(per):
+            back(k).wait_send()
+
+        def drained(mine, theirs):
+            for k, d in mine:
+                pass_on(k, d).wait_send()
+
+        by_core(drained)
+        for copy in sent:
+            copy.wait_send()
+        for q in range(max(chunks - 2, 0), chunks):
+            put(q).wait()
+
+    def end():
+        sent = []
+
+        def go(copy):
+            copy.start()
+            sent.append(copy)
+
+        for i in range(steps + 4):
+            if i < steps:
+                go(move(r, i, dev(zm, x), 2, first(i)))
+                if i >= late:
+                    go(move(r, i, dev(ze, xb), 0, first(i)))
+
+            def ship(mine, theirs):
+                for u, (k, d) in enumerate(mine):
+                    if turn(u) == i:
+                        unit(k, d, dev(zm, x)).start()
+
+            by_core(ship)
+            if i == 0:
+                load_sigma()
+            if i == late:
+                have_sigma()
+            for lag, zz in ((1, zm), (2, zo), (3, zf)):
+                j = i - lag
+                if late <= j < steps:
+                    b = at(zz, x)
+                    move(b, j, twin, 0).wait_recv()
+                    go(move(b, j, dev(ze, xb), 0))
+            for lag, zz in ((1, ze), (2, zm), (3, zo), (4, zf)):
+                j = i - lag
+                if late <= j < steps:
+                    move(at(zz, xb), j, twin, 0).wait_recv()
+            j = i - 4
+            if late <= j < steps:
+                multiply(j)
+                if j % split == split - 1:
+                    q = j // split
+                    finish(q, q - 2 if q - 2 >= spare else None)
+
+        def home(k):
+            where = pl.ds(k * tile, tile)
+            return pltpu.make_async_copy(ef.at[where], out.at[where, pl.ds(0, spare * wide)], e_send.at[k])
+
+        for k in range(per):
+            back(k).wait_recv()
+            home(k).start()
+        for k in range(per):
+            home(k).wait()
+
+        def drained(mine, theirs):
+            for k, d in mine:
+                unit(k, d, dev(zm, x)).wait_send()
+
+        by_core(drained)
+        for copy in sent:
+            copy.wait_send()
+        for q in range(max(chunks - 2, spare), chunks):
+            put(q).wait()
+
+    @pl.when(z == zm)
+    def _():
+        middle()
+
+    @pl.when(z == ze)
+    def _():
+        end()
+
+    each(0, held, lambda j: far(j).wait_send())
+
+    def share(k):
+        return pltpu.make_async_remote_copy(
+            src_ref=parts.at[r], dst_ref=parts.at[r], send_sem=v_send.at[k - 1], recv_sem=v_recv.at[k - 1],
+            device_id=(g, lax.rem(r + k, n), c), device_id_type=MESH)
+
+    def gone(k):
+        frm = lax.rem(r + n - k, n)
+        return pltpu.make_async_remote_copy(
+            src_ref=parts.at[frm], dst_ref=parts.at[frm], send_sem=v_send.at[k - 1], recv_sem=v_recv.at[k - 1],
+            device_id=(g, lax.rem(r + k, n), c), device_id_type=MESH)
+
+    each(1, n, lambda k: share(k).start())
+    each(1, n, lambda k: gone(k).wait_recv())
+    each(1, n, lambda k: share(k).wait_send())
+    total = parts[0]
+    for k in range(1, n):
+        total += parts[k]
+    sums[...] = total
+
+
+def plan(n, nc, per, tile, rows, cols):
+    if n != 8 or nc != 2 or rows != per * tile:
+        return None
+    wide, split, spare, kept = 256, 2, 2, 3
+    if cols % wide or cols // wide <= spare or per % split or kept > per or rows % nc:
+        return None
+    return wide, split, spare, kept
+
+
 def body(n, nc, sigma_anc, panel, holder, dinv_diag):
     tiles = holder.shape[0]
     rows, width = sigma_anc.shape
@@ -249,23 +661,11 @@
     ids = jnp.arange(tiles, dtype=jnp.int32)
     logical = jnp.sum(jnp.where(holder[:, None] == ids[None, :], ids[:, None], 0), axis=0, dtype=jnp.int32)
     dma = pltpu.SemaphoreType.DMA
-    out, sums = pl.pallas_call(
-        functools.partial(kernel, n, nc),
-        out_shape=(
-            jax.ShapeDtypeStruct((rows, cols), jnp.bfloat16),
-            jax.ShapeDtypeStruct((1, cols), jnp.float32),
-        ),
-        in_specs=[
-            pl.BlockSpec(memory_space=pltpu.SMEM),
-            pl.BlockSpec(memory_space=pltpu.SMEM),
-            pl.BlockSpec(memory_space=pl.ANY),
-            pl.BlockSpec(memory_space=pl.ANY),
-        ],
-        out_specs=(
-            pl.BlockSpec(memory_space=pl.ANY),
-            pl.BlockSpec(memory_space=pltpu.VMEM),
-        ),
-        scratch_shapes=[
+    form = plan(n, nc, per, tile, rows, cols)
+    if form is None:
+        call = functools.partial(kernel, n, nc)
+        limit = 60 << 20
+        scratch = [
             pltpu.VMEM((width * nc // tile, rows, tile), sigma_anc.dtype),
             pltpu.VMEM((tiles, tile, cols), panel.dtype),
             pltpu.VMEM((rows, cols), jnp.float32),
@@ -281,9 +681,62 @@
             dma((per,)),
             dma((n,)),
             dma((n,)),
+        ]
+    else:
+        wide, split, spare, kept = form
+        call = functools.partial(ladder, n, nc, *form)
+        limit = 63 << 20
+        chunks = cols // wide
+        steps = chunks * split
+        scratch = [
+            pltpu.VMEM((width * nc // tile, rows, tile), sigma_anc.dtype),
+            pltpu.VMEM((rows, wide), jnp.float32),
+            pltpu.VMEM((2, rows, wide), jnp.bfloat16),
+            pltpu.VMEM((rows, spare * wide), jnp.bfloat16),
+            pltpu.VMEM((tile, spare * wide), jnp.float32),
+            pltpu.VMEM((max(kept, 1), rows, tile), sigma_anc.dtype),
+            pltpu.VMEM((max(kept, 1), rows, tile), sigma_anc.dtype),
+            pltpu.VMEM((n, 1, cols), jnp.float32),
+            dma((2, width // tile)),
+            dma((width // tile,)),
+            dma((chunks,)),
+            dma((n, 3, steps)),
+            dma((n, steps)),
+            dma((per, n)),
+            dma((per, n)),
+            dma((per, n)),
+            dma((per, n)),
+            dma((2, max(kept, 1))),
+            dma((2, max(kept, 1))),
+            dma((2, max(kept, 1))),
+            dma((2, max(kept, 1))),
+            dma((per,)),
+            dma((per,)),
+            dma((chunks,)),
+            dma((n,)),
+            dma((n,)),
+        ]
+        scratch += [pltpu.VMEM((tiles, tile, wide), panel.dtype)] * chunks
+        scratch += [pltpu.VMEM((tile, width * nc), sigma_anc.dtype)] * per
+    out, sums = pl.pallas_call(
+        call,
+        out_shape=(
+            jax.ShapeDtypeStruct((rows, cols), jnp.bfloat16),
+            jax.ShapeDtypeStruct((1, cols), jnp.float32),
+        ),
+        in_specs=[
+            pl.BlockSpec(memory_space=pltpu.SMEM),
+            pl.BlockSpec(memory_space=pltpu.SMEM),
+            pl.BlockSpec(memory_space=pl.ANY),
+            pl.BlockSpec(memory_space=pl.ANY),
         ],
+        out_specs=(
+            pl.BlockSpec(memory_space=pl.ANY),
+            pl.BlockSpec(memory_space=pltpu.VMEM),
+        ),
+        scratch_shapes=scratch,
         compiler_params=pltpu.CompilerParams(
-            collective_id=0, has_side_effects=True, vmem_limit_bytes=60 << 20
+            collective_id=0, has_side_effects=True, vmem_limit_bytes=limit
         ),
     )(holder, logical, sigma_anc, panel.reshape(per, tile, cols))
     return out, dinv_diag + sums.reshape(cols)

time: 261 us -> 296 us (1.13)
  Pallas kernels: 253 us -> 289 us
    pallas_call x1, Pallas kernels: 253 us -> 289 us  [body(): pl.pallas_call(call, out_shape=(jax.ShapeDtypeStruct((rows, cols), jnp.bf...]
where the time goes in v1:
time: 296 us
  Pallas kernels  289 us (98%)
  local copies, waits for them, and re-layouts  3.76 us (1%)
    pallas_call x1, Pallas kernels, body(): pl.pallas_call(call, out_shape=(jax.ShapeDtypeStruct((rows, cols), jnp.bf...  289 us

profile of v1, /device:TPU:0, one launch (start us, length us, event | category | flops | bytes accessed | tf_op | source)
XLA Modules:
  0.0 296.1 jit_solution(4918453930561573104)
XLA Ops:
  0.6 1.3 select_reduce_fusion.logical
  1.9 0.0 copy-start
  1.9 289.1 %shard_map.59 = (bf16[1024,1536]{1,0:T(8,128)(2,1)}, f32[1,1536]{1,0:T(1,128)}) custom-call(s32[64]{0:T(128)} %holder.1, s32[64]{0:T(128)} %select_reduce_fusion.logical, bf16[1024,4096]{1,0:T(8,128)(2,1)} %sigma.1, bf16[8,128,1536]{2,1,0:T(8,128)(2,1)} %bitcast.1), custom_call_target="tpu_custom_call" | custom-call | tf_op jit(solution)/shard_map/pallas_call | solution.py:721
  291.0 0.7 reduce
  291.7 0.0 copy-done
  291.7 0.6 add.3
  292.3 3.8 %copy.7 = bf16[1024,1536]{1,0:T(8,128)(2,1)} copy(bf16[1024,1536]{1,0:T(8,128)(2,1)} %get-tuple-element.8) | data formatting | bytes 6291456
Async XLA Ops:
  1.9 289.8 %copy-start = (f32[1536]{0:T(1024)S(1)}, f32[1536]{0:T(1024)}, u32[]{:S(2)}) copy-start(f32[1536]{0:T(1024)} %param.7) | copy-start | bytes 18436

commit v2 on v0

--- a/solution.py
+++ b/solution.py
@@ -238,6 +238,442 @@
     sums[...] = total
 
 
+def ladder(n, nc, wide, table, fars, kept, lead, cap, stop, holder, logical, sigma, panel, out, sums,
+           s, acc, staged, ef, accf, across, along, parts,
+           far_sem, near_sem, own_sem, p_send, p_recv, u_send, u_recv, w_send, w_recv,
+           t_send, t_recv, y_send, y_recv, e_send, e_recv, o_sem, v_send, v_recv, *bufs):
+    g = lax.axis_index("groups")
+    r = lax.axis_index("row")
+    c = lax.axis_index("col")
+    per, tile, cols = panel.shape
+    rows, width = sigma.shape
+    chunks = cols // wide
+    ps, ses = bufs[:chunks], bufs[chunks:]
+    held = width // tile
+    steps = len(table)
+    final = {q: i for i, (q, _, _) in enumerate(table)}
+    near_edge = [i for i in range(steps) if table[i][0] not in fars]
+    z = r // 2
+    x = lax.rem(r, 2)
+    xb = 1 - x
+    side = z // 2
+    ze, zm, zo, zf = 3 * side, 1 + side, 2 - side, 3 - 3 * side
+    edge = 2 * ze + x
+
+    def at(zz, xx):
+        return 2 * zz + xx
+
+    def dev(zz, xx):
+        return (g, 2 * zz + xx, c)
+
+    twin = (g, r, 1 - c)
+
+    def own(q):
+        return pltpu.make_async_copy(
+            panel.at[:, :, pl.ds(q * wide, wide)], ps[q].at[pl.ds(r * per, per)], own_sem.at[q])
+
+    for q in range(chunks):
+        own(q).start()
+
+    barrier = pltpu.get_barrier_semaphore()
+
+    def greet(k, carry):
+        pl.semaphore_signal(barrier, 1, device_id=(g, lax.rem(r + k, n), c), device_id_type=MESH)
+        return carry
+
+    lax.fori_loop(1, n, greet, 0)
+    pl.semaphore_signal(barrier, 1, device_id=twin, device_id_type=MESH)
+    pl.semaphore_wait(barrier, n)
+
+    def each(low, high, act):
+        def step(k, carry):
+            act(k)
+            return carry
+        lax.fori_loop(low, high, step, 0)
+
+    def piece(block, i):
+        q, low, high = table[i]
+        return ps[q].at[pl.ds(block * per + low, high - low)]
+
+    def move(block, i, to, way):
+        return pltpu.make_async_remote_copy(
+            src_ref=piece(block, i), dst_ref=piece(block, i),
+            send_sem=p_send.at[block, way, i], recv_sem=p_recv.at[block, i],
+            device_id=to, device_id_type=MESH)
+
+    def near(j):
+        return pltpu.make_async_copy(
+            sigma.at[:, pl.ds(pl.multiple_of(j * tile, tile), tile)], s.at[c * held + j], near_sem.at[j])
+
+    def far(j):
+        return pltpu.make_async_remote_copy(
+            src_ref=sigma.at[:, pl.ds(pl.multiple_of(j * tile, tile), tile)], dst_ref=s.at[c * held + j],
+            send_sem=far_sem.at[0, j], recv_sem=far_sem.at[1, j], device_id=twin, device_id_type=MESH)
+
+    def far_landed(j):
+        t = (1 - c) * held + j
+        return pltpu.make_async_remote_copy(
+            src_ref=s.at[t], dst_ref=s.at[t],
+            send_sem=far_sem.at[0, j], recv_sem=far_sem.at[1, j], device_id=twin, device_id_type=MESH)
+
+    def load_sigma():
+        each(0, held, lambda j: far(j).start())
+        each(0, held, lambda j: near(j).start())
+
+    def have_sigma():
+        each(0, held, lambda j: near(j).wait())
+        each(0, held, lambda j: far_landed(j).wait_recv())
+        parts[r] = jnp.zeros((1, cols), jnp.float32)
+
+    rb = block_of(rows, 512)
+
+    def multiply(i):
+        q, low, high = table[i]
+        if low == 0:
+            acc[...] = jnp.zeros_like(acc)
+        downs = rows // rb
+
+        def block(u, carry):
+            pair = u // downs
+            rs = pl.ds(pl.multiple_of(lax.rem(u, downs) * rb, rb), rb)
+            slots = [(2 * pair + m) * per + j for m in range(2) for j in range(low, high)]
+            lhs = jnp.concatenate([s[logical[t], rs, :] for t in slots], axis=1)
+            rhs = jnp.concatenate([ps[q][t] for t in slots], axis=0)
+            acc[rs, :] += jnp.dot(lhs, rhs, preferred_element_type=jnp.float32)
+            return carry
+
+        lax.fori_loop(0, (n // 2) * downs, block, 0)
+
+    def put(q, nth):
+        return pltpu.make_async_copy(
+            staged.at[nth % 2], out.at[:, pl.ds(q * wide, wide)], o_sem.at[q])
+
+    def finish(q, mine):
+        cs = pl.ds(q * wide, wide)
+        nth = mine.index(q)
+        if nth >= 2:
+            put(mine[nth - 2], nth).wait()
+
+        def weigh(j, carry):
+            where = pl.ds(pl.multiple_of(j * tile, tile), tile)
+            prod = acc[where, :]
+            staged[nth % 2, where, :] = (-prod).astype(staged.dtype)
+            term = ps[q][holder[r * per + j]].astype(jnp.float32) * prod
+            parts[r, :, cs] += jnp.sum(term, axis=0, keepdims=True)
+            return carry
+
+        lax.fori_loop(0, per, weigh, 0)
+        put(q, nth).start()
+
+    def rel(idx):
+        zz = idx // 2
+        base = jnp.where(zz == 0, 1, jnp.where(zz == 1, 2, jnp.where(zz == 2, 0, 3)))
+        return 2 * (base + side * (3 - 2 * base)) + lax.rem(x + idx, 2)
+
+    units = [(k, d) for k in range(per) for d in range(1 if k >= kept else 3, n)]
+    halves = units[0::2], units[1::2]
+
+    def turn(u, group):
+        return 1 + u * (steps - 1 - stop) // len(group)
+
+    def strip(k, d):
+        low = k if d == 4 else 0
+        return pl.ds(rel(d) * per + low, per - low)
+
+    def unit(k, d, to):
+        return pltpu.make_async_remote_copy(
+            src_ref=s.at[strip(k, d), pl.ds(k * tile, tile)], dst_ref=ses[k].at[strip(k, d)],
+            send_sem=u_send.at[k, d], recv_sem=u_recv.at[k, d], device_id=to, device_id_type=MESH)
+
+    def pass_on(k, d):
+        ref = ses[k].at[strip(k, d)]
+        return pltpu.make_async_remote_copy(
+            src_ref=ref, dst_ref=ref, send_sem=w_send.at[k, d], recv_sem=w_recv.at[k, d],
+            device_id=twin, device_id_type=MESH)
+
+    def by_core(act):
+        @pl.when(c == 0)
+        def _():
+            act(halves[0], halves[1])
+
+        @pl.when(c != 0)
+        def _():
+            act(halves[1], halves[0])
+
+    half = rows // nc
+
+    def lend(k, way):
+        dst = (across, along)[way].at[k, pl.ds(pl.multiple_of(c * half, half), half)]
+        who = (at(ze, xb), at(zf, x))[way]
+        return pltpu.make_async_remote_copy(
+            src_ref=s.at[who * per + k, pl.ds(pl.multiple_of(c * half, half), half)], dst_ref=dst,
+            send_sem=t_send.at[way, k], recv_sem=t_recv.at[way, k],
+            device_id=(dev(zm, xb), dev(zo, x))[way], device_id_type=MESH)
+
+    def lend_on(k, way, core):
+        ref = (across, along)[way].at[k, pl.ds(pl.multiple_of(core * half, half), half)]
+        return pltpu.make_async_remote_copy(
+            src_ref=ref, dst_ref=ref, send_sem=y_send.at[way, k], recv_sem=y_recv.at[way, k],
+            device_id=twin, device_id_type=MESH)
+
+    def back(k, f):
+        where = pl.ds(k * tile, tile)
+        return pltpu.make_async_remote_copy(
+            src_ref=ef.at[f, where], dst_ref=out.at[where, pl.ds(fars[f] * wide, wide)], send_sem=e_send.at[k, f], recv_sem=e_recv.at[k, f],
+            device_id=dev(ze, x), device_id_type=MESH)
+
+    def edge_landed(k):
+        def landed(mine, theirs):
+            for kk, d in theirs:
+                if kk == k:
+                    pass_on(k, d).wait_recv()
+
+        by_core(landed)
+        if k < kept:
+            for way in range(2):
+                lend_on(k, way, 1 - c).wait_recv()
+
+    def for_edge(k, f):
+        q = fars[f]
+
+        def rhs(b):
+            return jnp.concatenate([ps[q][holder[b * per + j]] for j in range(per)], axis=0)
+
+        def turned(ref, b):
+            return lax.dot_general(
+                ref[...], rhs(b), (((0,), (0,)), ((), ())), preferred_element_type=jnp.float32)
+
+        accf[...] = turned(s.at[edge * per + k], r)
+        if k < kept:
+            accf[...] += turned(across.at[k], at(zm, xb))
+            accf[...] += turned(along.at[k], at(zo, x))
+
+        def straight(d, carry):
+            b = rel(d)
+            lhs = jnp.concatenate([ses[k][b * per + j] for j in range(per)], axis=1)
+            accf[...] += jnp.dot(lhs, rhs(b), preferred_element_type=jnp.float32)
+            return carry
+
+        lax.fori_loop(3 if k < kept else 1, 4, straight, 0)
+        lax.fori_loop(5, n, straight, 0)
+        lhs = jnp.concatenate(
+            [ses[j][edge * per + k].T for j in range(k)] + [ses[k][edge * per + j] for j in range(k, per)], axis=1)
+        accf[...] += jnp.dot(lhs, rhs(edge), preferred_element_type=jnp.float32)
+        ef[f, pl.ds(k * tile, tile), :] = (-accf[...]).astype(ef.dtype)
+        cs = pl.ds(q * wide, wide)
+        term = ps[q][holder[edge * per + k]].astype(jnp.float32) * accf[...]
+        parts[r, :, cs] += jnp.sum(term, axis=0, keepdims=True)
+        back(k, f).start()
+
+    def share(k):
+        return pltpu.make_async_remote_copy(
+            src_ref=parts.at[r], dst_ref=parts.at[r], send_sem=v_send.at[k - 1], recv_sem=v_recv.at[k - 1],
+            device_id=(g, lax.rem(r + k, n), c), device_id_type=MESH)
+
+    def gone(k):
+        frm = lax.rem(r + n - k, n)
+        return pltpu.make_async_remote_copy(
+            src_ref=parts.at[frm], dst_ref=parts.at[frm], send_sem=v_send.at[k - 1], recv_sem=v_recv.at[k - 1],
+            device_id=(g, lax.rem(r + k, n), c), device_id_type=MESH)
+
+    def middle():
+        sent = []
+
+        def go(copy):
+            copy.start()
+            sent.append(copy)
+
+        ready = {}
+        fixed = []
+        for k in range(per):
+            last = max(turn(max(u for u, (kk, _) in enumerate(lst) if kk == k), lst) for lst in halves)
+            fixed.append(max(last + 2, 5 + k if k < kept else 0))
+        busy = {}
+        for f, q in enumerate(fars):
+            for k in range(per):
+                i = max(fixed[k], final[q] + 3)
+                while busy.get(i, 0) >= cap and i < steps + 1:
+                    i += 1
+                busy[i] = busy.get(i, 0) + 1
+                ready.setdefault(i, []).append((k, f))
+        fresh = set(range(per))
+        total = max(steps + 2, max(ready) + 1)
+
+        def give(i):
+            if table[i][1] == 0:
+                own(table[i][0]).wait()
+            go(move(r, i, dev(zm, xb), 0))
+            go(move(r, i, dev(zo, x), 1))
+            if i in near_edge:
+                go(move(r, i, dev(ze, x), 2))
+
+        give(0)
+        for i in range(total):
+            if i + 1 < steps:
+                give(i + 1)
+            if i == 0:
+                load_sigma()
+            if i == 2:
+                have_sigma()
+            if i < steps:
+                b = at(ze, x)
+                move(b, i, twin, 0).wait_recv()
+                go(move(b, i, dev(zm, xb), 0))
+                go(move(b, i, dev(zo, x), 1))
+                b = at(zm, xb)
+                move(b, i, twin, 0).wait_recv()
+                go(move(b, i, dev(zo, x), 1))
+                b = at(zo, x)
+                move(b, i, twin, 0).wait_recv()
+                if i in near_edge:
+                    go(move(b, i, dev(ze, x), 2))
+            j = i - 1
+            if 0 <= j < steps:
+                b = at(zf, x)
+                move(b, j, twin, 0).wait_recv()
+                go(move(b, j, dev(zm, xb), 0))
+                if j in near_edge:
+                    go(move(b, j, dev(ze, x), 2))
+                move(at(ze, xb), j, twin, 0).wait_recv()
+                move(at(zo, xb), j, twin, 0).wait_recv()
+            for k in range(kept):
+                if i == 3 + k:
+                    for way in range(2):
+                        go(lend(k, way))
+                if i == 4 + k:
+                    for way in range(2):
+                        lend(k, way).wait_recv()
+                        go(lend_on(k, way, c))
+            j = i - 2
+
+            def relay(mine, theirs):
+                for u, (k, d) in enumerate(mine):
+                    if turn(u, mine) == j:
+                        unit(k, d, twin).wait_recv()
+                        pass_on(k, d).start()
+
+            by_core(relay)
+            for k, f in ready.get(i, ()):
+                if k in fresh:
+                    fresh.remove(k)
+                    edge_landed(k)
+                for_edge(k, f)
+            j = i - 2
+            if 0 <= j < steps:
+                move(at(zf, xb), j, twin, 0).wait_recv()
+                multiply(j)
+                if final[table[j][0]] == j:
+                    finish(table[j][0], list(range(chunks)))
+
+        each(1, n, lambda k: share(k).start())
+        for k in range(per):
+            for f in range(len(fars)):
+                back(k, f).wait_send()
+
+        def drained(mine, theirs):
+            for k, d in mine:
+                pass_on(k, d).wait_send()
+
+        by_core(drained)
+        for copy in sent:
+            copy.wait_send()
+        for q in range(max(chunks - 2, 0), chunks):
+            put(q, q).wait()
+
+    def end():
+        sent = []
+        mine = [q for q in range(chunks) if q not in fars]
+
+        def go(copy):
+            copy.start()
+            sent.append(copy)
+
+        def give(i):
+            if table[i][1] == 0:
+                own(table[i][0]).wait()
+            go(move(r, i, dev(zm, x), 2))
+            if i in near_edge:
+                go(move(r, i, dev(ze, xb), 0))
+
+        for i in range(min(lead, steps)):
+            give(i)
+        for i in range(steps + 3):
+            if i + lead < steps:
+                give(i + lead)
+
+            def ship(units, theirs):
+                for u, (k, d) in enumerate(units):
+                    if turn(u, units) == i:
+                        unit(k, d, dev(zm, x)).start()
+
+            if i == 0:
+                load_sigma()
+            if i == 1:
+                have_sigma()
+            by_core(ship)
+            for lag, zz in ((0, zm), (1, zo), (2, zf)):
+                j = i - lag
+                if j in near_edge:
+                    b = at(zz, x)
+                    move(b, j, twin, 0).wait_recv()
+                    go(move(b, j, dev(ze, xb), 0))
+            for lag, zz in ((0, ze), (1, zm), (2, zo), (3, zf)):
+                j = i - lag
+                if j in near_edge:
+                    move(at(zz, xb), j, twin, 0).wait_recv()
+            j = i - 3
+            if j in near_edge:
+                multiply(j)
+                if final[table[j][0]] == j:
+                    finish(table[j][0], mine)
+
+        each(1, n, lambda k: share(k).start())
+        for k in range(per):
+            for f in range(len(fars)):
+                back(k, f).wait_recv()
+
+        def drained(mine, theirs):
+            for k, d in mine:
+                unit(k, d, dev(zm, x)).wait_send()
+
+        by_core(drained)
+        for copy in sent:
+            copy.wait_send()
+        for nth in range(max(len(mine) - 2, 0), len(mine)):
+            put(mine[nth], nth).wait()
+
+    @pl.when(z == zm)
+    def _():
+        middle()
+
+    @pl.when(z == ze)
+    def _():
+        end()
+
+    each(0, held, lambda j: far(j).wait_send())
+
+    each(1, n, lambda k: gone(k).wait_recv())
+    each(1, n, lambda k: share(k).wait_send())
+    total = parts[0]
+    for k in range(1, n):
+        total += parts[k]
+    sums[...] = total
+
+
+def plan(n, nc, per, tile, rows, cols):
+    if n != 8 or nc != 2 or rows != per * tile:
+        return None
+    wide, fars, kept, lead, cap, stop = 256, (1, 3), 1, 2, 2, 0
+    chunks = cols // wide
+    if cols % wide or chunks <= max(fars) + 1 or per % 4 or kept > per or rows % nc:
+        return None
+    table = []
+    for q in range(chunks):
+        parts = 4 if q == chunks - 1 else 2
+        table += [(q, h * per // parts, (h + 1) * per // parts) for h in range(parts)]
+    return wide, tuple(table), fars, kept, lead, cap, stop
+
+
 def body(n, nc, sigma_anc, panel, holder, dinv_diag):
     tiles = holder.shape[0]
     rows, width = sigma_anc.shape
@@ -249,23 +685,11 @@
     ids = jnp.arange(tiles, dtype=jnp.int32)
     logical = jnp.sum(jnp.where(holder[:, None] == ids[None, :], ids[:, None], 0), axis=0, dtype=jnp.int32)
     dma = pltpu.SemaphoreType.DMA
-    out, sums = pl.pallas_call(
-        functools.partial(kernel, n, nc),
-        out_shape=(
-            jax.ShapeDtypeStruct((rows, cols), jnp.bfloat16),
-            jax.ShapeDtypeStruct((1, cols), jnp.float32),
-        ),
-        in_specs=[
-            pl.BlockSpec(memory_space=pltpu.SMEM),
-            pl.BlockSpec(memory_space=pltpu.SMEM),
-            pl.BlockSpec(memory_space=pl.ANY),
-            pl.BlockSpec(memory_space=pl.ANY),
-        ],
-        out_specs=(
-            pl.BlockSpec(memory_space=pl.ANY),
-            pl.BlockSpec(memory_space=pltpu.VMEM),
-        ),
-        scratch_shapes=[
+    form = plan(n, nc, per, tile, rows, cols)
+    if form is None:
+        call = functools.partial(kernel, n, nc)
+        limit = 60 << 20
+        scratch = [
             pltpu.VMEM((width * nc // tile, rows, tile), sigma_anc.dtype),
             pltpu.VMEM((tiles, tile, cols), panel.dtype),
             pltpu.VMEM((rows, cols), jnp.float32),
@@ -281,9 +705,62 @@
             dma((per,)),
             dma((n,)),
             dma((n,)),
+        ]
+    else:
+        wide, table, fars, kept = form[:4]
+        call = functools.partial(ladder, n, nc, *form)
+        limit = 63 << 20
+        chunks = cols // wide
+        steps = len(table)
+        scratch = [
+            pltpu.VMEM((width * nc // tile, rows, tile), sigma_anc.dtype),
+            pltpu.VMEM((rows, wide), jnp.float32),
+            pltpu.VMEM((2, rows, wide), jnp.bfloat16),
+            pltpu.VMEM((len(fars), rows, wide), jnp.bfloat16),
+            pltpu.VMEM((tile, wide), jnp.float32),
+            pltpu.VMEM((max(kept, 1), rows, tile), sigma_anc.dtype),
+            pltpu.VMEM((max(kept, 1), rows, tile), sigma_anc.dtype),
+            pltpu.VMEM((n, 1, cols), jnp.float32),
+            dma((2, width // tile)),
+            dma((width // tile,)),
+            dma((chunks,)),
+            dma((n, 3, steps)),
+            dma((n, steps)),
+            dma((per, n)),
+            dma((per, n)),
+            dma((per, n)),
+            dma((per, n)),
+            dma((2, max(kept, 1))),
+            dma((2, max(kept, 1))),
+            dma((2, max(kept, 1))),
+            dma((2, max(kept, 1))),
+            dma((per, len(fars))),
+            dma((per, len(fars))),
+            dma((chunks,)),
+            dma((n,)),
+            dma((n,)),
+        ]
+        scratch += [pltpu.VMEM((tiles, tile, wide), panel.dtype)] * chunks
+        scratch += [pltpu.VMEM((tiles, tile, tile), sigma_anc.dtype)] * per
+    out, sums = pl.pallas_call(
+        call,
+        out_shape=(
+            jax.ShapeDtypeStruct((rows, cols), jnp.bfloat16),
+            jax.ShapeDtypeStruct((1, cols), jnp.float32),
+        ),
+        in_specs=[
+            pl.BlockSpec(memory_space=pltpu.SMEM),
+            pl.BlockSpec(memory_space=pltpu.SMEM),
+            pl.BlockSpec(memory_space=pl.ANY),
+            pl.BlockSpec(memory_space=pl.ANY),
         ],
+        out_specs=(
+            pl.BlockSpec(memory_space=pl.ANY),
+            pl.BlockSpec(memory_space=pltpu.VMEM),
+        ),
+        scratch_shapes=scratch,
         compiler_params=pltpu.CompilerParams(
-            collective_id=0, has_side_effects=True, vmem_limit_bytes=60 << 20
+            collective_id=0, has_side_effects=True, vmem_limit_bytes=limit
         ),
     )(holder, logical, sigma_anc, panel.reshape(per, tile, cols))
     return out, dinv_diag + sums.reshape(cols)

time: 261 us -> 252 us (0.966)
  Pallas kernels: 253 us -> 244 us
    pallas_call x1, Pallas kernels: 253 us -> 244 us  [body(): pl.pallas_call(call, out_shape=(jax.ShapeDtypeStruct((rows, cols), jnp.bf...]
where the time goes in v2:
time: 252 us; the launch traced here: 251 us
  Pallas kernels  244 us (97%)
  local copies, waits for them, and re-layouts  3.76 us (1%)
  other arithmetic  2.58 us (1%)
    pallas_call x1, Pallas kernels, body(): pl.pallas_call(call, out_shape=(jax.ShapeDtypeStruct((rows, cols), jnp.bf...  244 us

profile of v2, /device:TPU:0, one launch (start us, length us, event | category | flops | bytes accessed | tf_op | source)
XLA Modules:
  0.0 251.4 jit_solution(13621014946380477170)
XLA Ops:
  0.6 1.3 select_reduce_fusion.logical
  1.9 0.0 copy-start
  1.9 244.4 %shard_map.59 = (bf16[1024,1536]{1,0:T(8,128)(2,1)}, f32[1,1536]{1,0:T(1,128)}) custom-call(s32[64]{0:T(128)} %holder.1, s32[64]{0:T(128)} %select_reduce_fusion.logical, bf16[1024,4096]{1,0:T(8,128)(2,1)} %sigma.1, bf16[8,128,1536]{2,1,0:T(8,128)(2,1)} %bitcast.1), custom_call_target="tpu_custom_call" | custom-call | tf_op jit(solution)/shard_map/pallas_call | solution.py:745
  246.3 0.7 reduce
  247.0 0.0 copy-done
  247.1 0.6 add.3
  247.7 3.8 %copy.7 = bf16[1024,1536]{1,0:T(8,128)(2,1)} copy(bf16[1024,1536]{1,0:T(8,128)(2,1)} %get-tuple-element.8) | data formatting | bytes 6291456
Async XLA Ops:
  1.9 245.2 %copy-start = (f32[1536]{0:T(1024)S(1)}, f32[1536]{0:T(1024)}, u32[]{:S(2)}) copy-start(f32[1536]{0:T(1024)} %param.7) | copy-start | bytes 18436

commit v3 on v2

--- a/solution.py
+++ b/solution.py
@@ -663,7 +663,7 @@
 def plan(n, nc, per, tile, rows, cols):
     if n != 8 or nc != 2 or rows != per * tile:
         return None
-    wide, fars, kept, lead, cap, stop = 256, (1, 3), 1, 2, 2, 0
+    wide, fars, kept, lead, cap, stop = 256, (1, 3), 0, 2, 2, 0
     chunks = cols // wide
     if cols % wide or chunks <= max(fars) + 1 or per % 4 or kept > per or rows % nc:
         return None

time: 252 us -> 250 us (level)
  no operation moved by 1% of the time
where the time goes in v3:
time: 250 us; the launch traced here: 249 us
  Pallas kernels  242 us (97%)
  local copies, waits for them, and re-layouts  3.76 us (2%)
  other arithmetic  2.58 us (1%)
    pallas_call x1, Pallas kernels, body(): pl.pallas_call(call, out_shape=(jax.ShapeDtypeStruct((rows, cols), jnp.bf...  242 us

profile of v3, /device:TPU:0, one launch (start us, length us, event | category | flops | bytes accessed | tf_op | source)
XLA Modules:
  0.0 249.2 jit_solution(16315099172636060148)
XLA Ops:
  0.6 1.3 select_reduce_fusion.logical
  1.9 0.0 copy-start
  1.9 242.3 %shard_map.59 = (bf16[1024,1536]{1,0:T(8,128)(2,1)}, f32[1,1536]{1,0:T(1,128)}) custom-call(s32[64]{0:T(128)} %holder.1, s32[64]{0:T(128)} %select_reduce_fusion.logical, bf16[1024,4096]{1,0:T(8,128)(2,1)} %sigma.1, bf16[8,128,1536]{2,1,0:T(8,128)(2,1)} %bitcast.1), custom_call_target="tpu_custom_call" | custom-call | tf_op jit(solution)/shard_map/pallas_call | solution.py:745
  244.2 0.7 reduce
  244.9 0.0 copy-done
  244.9 0.6 add.3
  245.5 3.8 %copy.7 = bf16[1024,1536]{1,0:T(8,128)(2,1)} copy(bf16[1024,1536]{1,0:T(8,128)(2,1)} %get-tuple-element.8) | data formatting | bytes 6291456
Async XLA Ops:
  1.9 243.0 %copy-start = (f32[1536]{0:T(1024)S(1)}, f32[1536]{0:T(1024)}, u32[]{:S(2)}) copy-start(f32[1536]{0:T(1024)} %param.7) | copy-start | bytes 18436

commit v4 on v3

--- a/solution.py
+++ b/solution.py
@@ -663,7 +663,7 @@
 def plan(n, nc, per, tile, rows, cols):
     if n != 8 or nc != 2 or rows != per * tile:
         return None
-    wide, fars, kept, lead, cap, stop = 256, (1, 3), 0, 2, 2, 0
+    wide, fars, kept, lead, cap, stop = 256, (0, 3), 0, 2, 2, 0
     chunks = cols // wide
     if cols % wide or chunks <= max(fars) + 1 or per % 4 or kept > per or rows % nc:
         return None

time: 250 us -> 250 us (level)
  no operation moved by 1% of the time
where the time goes in v4:
time: 250 us; the launch traced here: 249 us
  Pallas kernels  242 us (97%)
  local copies, waits for them, and re-layouts  3.76 us (2%)
  other arithmetic  2.58 us (1%)
    pallas_call x1, Pallas kernels, body(): pl.pallas_call(call, out_shape=(jax.ShapeDtypeStruct((rows, cols), jnp.bf...  242 us

profile of v4, /device:TPU:0, one launch (start us, length us, event | category | flops | bytes accessed | tf_op | source)
XLA Modules:
  0.0 249.2 jit_solution(6688238126472985288)
XLA Ops:
  0.6 1.3 select_reduce_fusion.logical
  1.9 0.0 copy-start
  1.9 242.3 %shard_map.59 = (bf16[1024,1536]{1,0:T(8,128)(2,1)}, f32[1,1536]{1,0:T(1,128)}) custom-call(s32[64]{0:T(128)} %holder.1, s32[64]{0:T(128)} %select_reduce_fusion.logical, bf16[1024,4096]{1,0:T(8,128)(2,1)} %sigma.1, bf16[8,128,1536]{2,1,0:T(8,128)(2,1)} %bitcast.1), custom_call_target="tpu_custom_call" | custom-call | tf_op jit(solution)/shard_map/pallas_call | solution.py:745
  244.2 0.7 reduce
  244.9 0.0 copy-done
  244.9 0.6 add.3
  245.5 3.8 %copy.7 = bf16[1024,1536]{1,0:T(8,128)(2,1)} copy(bf16[1024,1536]{1,0:T(8,128)(2,1)} %get-tuple-element.8) | data formatting | bytes 6291456
Async XLA Ops:
  1.9 243.0 %copy-start = (f32[1536]{0:T(1024)S(1)}, f32[1536]{0:T(1024)}, u32[]{:S(2)}) copy-start(f32[1536]{0:T(1024)} %param.7) | copy-start | bytes 18436
